TPU v7x, 1024 devices: a whole 4x4x32 slice. The times are simulated.
1024 devices in a mesh: fsdp: 8 (over x, core), tensor: 128 (over z, y).
Axes of the slice: x: 4, y: 4, z: 32, core: 2. Of those that a mesh axis runs over, the one named last changes fastest.
Arguments:
- weight: bfloat16 [14336, 4096], P('tensor', 'fsdp'), may hold values from -0.0017929077 to 0.0017929077
- momentum: float32 [14336, 4096], P('tensor', 'fsdp'), may hold values from -18 to 18
- grad: bfloat16 [14336, 4096], P('tensor', 'fsdp'), may hold values from -6 to 6
- q_prev: float32 [14336, 256], P('tensor'), may hold values from -0.046875 to 0.046875
Outputs:
- new_weight: bfloat16 [14336, 4096], P('tensor', 'fsdp')
- new_momentum: float32 [14336, 4096], P('tensor', 'fsdp')
- q_new: float32 [14336, 256], P('tensor')
All inputs are finite; a program needn't handle non-finite values.
Results may differ from a plain program's by a relative error of at most 0.001.
Values sent between devices are 32-bit elements; how exact they have to be, the bound alone decides.
A program may use at most 32 MiB of HBM per device.

v0:
```python
import functools
import math

import jax
import jax.numpy as jnp
from jax import lax
from jax.sharding import Mesh
from jax.sharding import PartitionSpec as P

TENSOR = ("tensor_0", "tensor_1")


momentum_decay = 0.95
step_rate = 0.02
norm_eps = 1e-06


def sum_by_axis(total, axes):
    for axis in axes:
        total = lax.psum_scatter(total, axis, scatter_dimension=0, tiled=True)
    return total


def whole_of(x, axes, dim):
    whole = x
    for number in range(len(axes) - 1, -1, -1):
        whole = lax.all_gather(whole, axes[number], axis=dim, tiled=True)
    return whole


def gathered_total(x, axis):
    blocks = lax.all_gather(x, axis)
    return blocks.sum(axis=0)


def by_axis(x, axes):
    return functools.reduce(lax.psum, axes, x)


def contract_first(left, right):
    return lax.dot_general(
        left,
        right,
        (((0,), (0,)), ((), ())),
        precision=lax.Precision.HIGHEST,
        preferred_element_type=jnp.float32,
    )


def right_solve(lower, values):
    return jax.scipy.linalg.solve_triangular(lower, values.T, lower=True).T


def per_device(weight, momentum, grad, q_prev):
    highest = lax.Precision.HIGHEST
    buffer = momentum + grad.astype(jnp.float32)
    cols_here = buffer.shape[0]
    rows_here = buffer.shape[1]
    factor = step_rate * math.sqrt(
        cols_here * lax.axis_size(TENSOR) / (rows_here * lax.axis_size("fsdp"))
    )
    pieces = sum_by_axis(contract_first(buffer, q_prev), TENSOR)
    raw = whole_of(pieces, TENSOR, 0)
    local_gram = contract_first(raw, raw)
    local_cross = jnp.dot(buffer, raw, precision=highest, preferred_element_type=jnp.float32)
    gram, cross = (gathered_total(local_gram, "fsdp"), gathered_total(local_cross, "fsdp"))
    lower = jnp.linalg.cholesky(gram)
    ortho = right_solve(lower, raw)
    right = right_solve(lower, cross)
    column_sq = by_axis(jnp.sum(right * right, axis=0), TENSOR)
    q_new = right / (jnp.sqrt(column_sq) + norm_eps)
    new_momentum = buffer - (1.0 - momentum_decay) * lax.dot_general(
        right,
        ortho,
        (((1,), (1,)), ((), ())),
        precision=highest,
        preferred_element_type=jnp.float32,
    )
    update = lax.dot_general(
        q_new,
        ortho,
        (((1,), (1,)), ((), ())),
        precision=highest,
        preferred_element_type=jnp.float32,
    )
    new_weight = (weight.astype(jnp.float32) - factor * update).astype(jnp.bfloat16)
    return (new_weight, new_momentum, q_new)


def solution(mesh):
    torus = Mesh(mesh.devices.reshape(mesh.shape["fsdp"], 32, 4), ("fsdp", "tensor_0", "tensor_1"))
    return jax.shard_map(
        per_device,
        mesh=torus,
        in_specs=(P(TENSOR, "fsdp"), P(TENSOR, "fsdp"), P(TENSOR, "fsdp"), P(TENSOR, None)),
        out_specs=(P(TENSOR, "fsdp"), P(TENSOR, "fsdp"), P(TENSOR, None)),
        check_vma=False,
    )
```

profile of v0, /device:TPU:4, one launch (start us, length us, event | category | flops | bytes accessed | tf_op | source)
XLA Modules:
  0.0 421.5 jit_solution(9668790668453315600)
XLA Ops:
  7.2 0.8 copy-done
  8.1 2.4 fusion.7
  10.6 1.3 dynamic-slice.3
  12.5 141.4 %reduce-scatter.2.cloned.1.call-done = f32[16,256]{1,0:T(8,128)} async-done(((f32[512,256]{1,0:T(8,128)}), f32[16,256]{1,0:T(8,128)}) %reduce-scatter.2.cloned.1.call-update) | async-done | bytes 16400 | tf_op jit(solution)/shard_map/reduce_scatter | solution.py:20
  153.9 17.5 %all-reduce.1 = f32[16,256]{1,0:T(8,128)S(1)} all-reduce(f32[16,256]{1,0:T(8,128)} %reduce-scatter.2.cloned.1.call-done), channel_id=5, replica_groups=mesh['fsdp'=8,'tensor_0'=32,'tensor_1'=4] {'tensor_1'}, use_global_device_ids=true, to_apply=%region_1.0.clone | all-reduce | flops 4096 | bytes 32768
  171.4 12.0 %all-gather.2 = f32[4,4,256]{2,1,0:T(4,128)S(1)} all-gather(f32[1,4,256]{2,1,0:T(4,128)S(1)} %dynamic-slice_bitcast_fusion), channel_id=1, replica_groups=mesh['fsdp'=8,'tensor_0'=32,'tensor_1'=4] {'tensor_1'}, dimensions={0}, use_global_device_ids=true | all-gather | bytes 20480 | tf_op jit(solution)/shard_map/all_gather | solution.py:27
  183.4 55.5 %all_gather.19 = f32[512,256]{1,0:T(8,128)S(1)} all-gather(f32[16,256]{1,0:T(8,128)S(1)} %reshape.54), channel_id=1, replica_groups=mesh['fsdp'=8,'tensor_0'=32,'tensor_1'=4] {'tensor_0'}, dimensions={0}, use_global_device_ids=true | all-gather | bytes 540672 | tf_op jit(solution)/shard_map/all_gather | solution.py:27
  238.9 1.7 fusion.23
  241.2 12.6 %all-gather.1 = f32[896,256]{1,0:T(8,128)S(1)} all-gather(f32[112,256]{1,0:T(8,128)S(1)} %fusion.6), channel_id=3, replica_groups=mesh['fsdp'=8,'tensor_0'=32,'tensor_1'=4] {'fsdp'}, dimensions={0}, use_global_device_ids=true | all-gather | bytes 1032192 | tf_op jit(solution)/shard_map/all_gather | solution.py:32
  253.8 24.8 %all-gather.5.cloned.1.call-done = f32[2048,256]{1,0:T(8,128)} async-done(((f32[256,256]{1,0:T(8,128)}), f32[2048,256]{1,0:T(8,128)}) %all-gather.5.cloned.1.call-update) | async-done | bytes 2097168 | tf_op jit(solution)/shard_map/all_gather | solution.py:32
  278.6 1.8 reduce_sum.27
  280.6 11.7 %cholesky.50 = f32[128,128]{1,0:T(8,128)S(1)} custom-call(f32[128,128]{1,0:T(8,128)S(1)} %cholesky.118), custom_call_target="Cholesky" | custom-call | tf_op jit(solution)/shard_map/jit(cholesky)/cholesky | solution.py:67
  292.4 9.8 %custom-call.18 = f32[1,128,128]{1,2,0:T(8,128)S(1)} custom-call(f32[1,128,128]{2,1,0:T(8,128)S(1)} %get-tuple-element.24), custom_call_target="InvertDiagBlocksLowerTriangular" | custom-call | tf_op jit(solution)/shard_map/jit(cholesky)/cholesky | solution.py:67
  302.6 11.7 %cholesky.105 = f32[128,128]{1,0:T(8,128)S(1)} custom-call(f32[128,128]{1,0:T(8,128)S(1)} %convolution_subtract_fusion.1), custom_call_target="Cholesky" | custom-call | tf_op jit(solution)/shard_map/jit(cholesky)/cholesky | solution.py:67
  314.4 0.6 compare_reduce_fusion
  316.4 4.2 while.1
  317.2 1.4 bitcast_dynamic-update-slice_fusion.2
  319.2 1.4 bitcast_dynamic-update-slice_fusion.2
  320.6 19.7 %custom-call.19 = f32[2,128,128]{1,2,0:T(8,128)S(1)} custom-call(f32[2,128,128]{2,1,0:T(8,128)S(1)} %get-tuple-element.10), custom_call_target="InvertDiagBlocksLowerTriangular" | custom-call | tf_op jit(solution)/shard_map/jit(_solve_triangular)/triangular_solve | solution.py:51
  341.0 58.9 %psum.14 = f32[256]{0:T(256)S(1)} all-reduce(f32[256]{0:T(256)S(1)} %multiply_reduce_fusion), channel_id=1, replica_groups=mesh['fsdp'=8,'tensor_0'=32,'tensor_1'=4] {'tensor_0'}, use_global_device_ids=true, to_apply=%region_9.10 | all-reduce | flops 256 | bytes 2048 | tf_op jit(solution)/shard_map/psum | solution.py:37
  399.9 10.5 %psum.15 = f32[256]{0:T(256)S(1)} all-reduce(f32[256]{0:T(256)S(1)} %psum.14), channel_id=1, replica_groups=mesh['fsdp'=8,'tensor_0'=32,'tensor_1'=4] {'tensor_1'}, use_global_device_ids=true, to_apply=%region_10.11 | all-reduce | flops 256 | bytes 2048 | tf_op jit(solution)/shard_map/psum | solution.py:37
  410.4 0.7 fusion.18
  412.5 1.1 fusion
  413.6 1.1 fusion.2
  (39 shorter events, 4.8 us)
Async XLA Ops:
  7.2 0.9 copy-start
  7.2 233.5 %copy-start.1 = (f32[112,512]{1,0:T(8,128)S(1)}, f32[112,512]{1,0:T(8,128)}, u32[]{:S(2)}) copy-start(f32[112,512]{1,0:T(8,128)} %param.5) | copy-start | bytes 688132
  7.2 233.5 %copy-start.2 = (bf16[112,512]{1,0:T(8,128)(2,1)S(1)}, bf16[112,512]{1,0:T(8,128)(2,1)}, u32[]{:S(2)}) copy-start(bf16[112,512]{1,0:T(8,128)(2,1)} %param.6) | copy-start | bytes 344068
  7.2 146.7 %reduce-scatter.2.cloned.1.call-start = ((), (), s32[]{:S(2)}) async-start(), calls=%async_computation.1 | async-start | bytes 540672 | tf_op jit(solution)/shard_map/reduce_scatter | solution.py:20
  10.5 268.1 %all-gather.5.cloned.1.call-start = ((), (), s32[]{:S(2)}) async-start(), calls=%async_computation.2 | async-start | bytes 2359296 | tf_op jit(solution)/shard_map/all_gather | solution.py:32
  340.3 73.3 %copy-start.3 = (bf16[112,512]{1,0:T(8,128)(2,1)S(1)}, bf16[112,512]{1,0:T(8,128)(2,1)}, u32[]{:S(2)}) copy-start(bf16[112,512]{1,0:T(8,128)(2,1)} %param.4) | copy-start | bytes 344068
Sparse Core Ops, SparseCore 0:
  11.4 142.4 reduce-scatter.1
  240.8 37.7 all-gather.4
where the time goes:
time: 422 us
  blocking collectives  167 us (40%)
  waiting for transfers between devices  166 us (39%)
  other arithmetic  56.2 us (13%)
  between operations  16.2 us (4%)
  matrix products  9.33 us (2%)
  local copies, waits for them, and re-layouts  6.31 us (1%)
    reduce_scatter x1, waiting for transfers between devices, sum_by_axis(): total = lax.psum_scatter(total, axis, scatter_dimension=0, tiled=True)  141 us
    psum x2, blocking collectives, by_axis(): return functools.reduce(lax.psum, axes, x)  69.4 us
    all_gather x2, blocking collectives, whole_of(): whole = lax.all_gather(whole, axes[number], axis=dim, tiled=True)  67.5 us
    another operation x6, other arithmetic, per_device(): lower = jnp.linalg.cholesky(gram)  33.9 us
    all_gather x1, waiting for transfers between devices, gathered_total(): blocks = lax.all_gather(x, axis)  24.8 us
    another operation x3, other arithmetic, right_solve(): return jax.scipy.linalg.solve_triangular(lower, values.T, lower=True).T  19.7 us
    unnamed x1, blocking collectives  17.5 us
    all_gather x1, blocking collectives, gathered_total(): blocks = lax.all_gather(x, axis)  12.6 us
  transfers between devices with their start and end apart: 2, of which 2 were waited for; matrix products, arithmetic and copies ran while one was open for 0% of the time, Pallas kernels for 0%

commit v1 on v0

v1 whole, which is shorter than its diff:
```python
import functools
import math

import jax
import jax.numpy as jnp
from jax import lax
from jax.experimental import pallas as pl
from jax.experimental.pallas import tpu as pltpu
from jax.sharding import Mesh
from jax.sharding import PartitionSpec as P

TENSOR = ("zf", "zn", "y")
MESH_ID = pl.DeviceIdType.MESH
TILES = 128
GRAM_TILES = 48
CROSS_TILES = 32

momentum_decay = 0.95
step_rate = 0.02
norm_eps = 1e-06


def dot(left, right, dims):
    return lax.dot_general(
        left,
        right,
        (dims, ((), ())),
        precision=lax.Precision.HIGHEST,
        preferred_element_type=jnp.float32,
    )


def far_first(n):
    return sorted(range(1, n), key=lambda d: -min(d, n - d)) + [0]


def remote(src, dst, send, recv, device):
    copy = pltpu.make_async_remote_copy(
        src_ref=src,
        dst_ref=dst,
        send_sem=send,
        recv_sem=recv,
        device_id=device,
        device_id_type=MESH_ID,
    )
    copy.start()


def drain(ref, sem):
    pltpu.make_async_copy(ref, ref, sem).wait()


def greet(axes):
    barrier = pltpu.get_barrier_semaphore()
    count = 0
    for axis, n in axes:
        me = lax.axis_index(axis)
        for d in range(1, n):
            pl.semaphore_signal(
                barrier, inc=1, device_id={axis: (me + d) % n}, device_id_type=MESH_ID
            )
            count += 1
    pl.semaphore_wait(barrier, count)


def sum_over(axis, n, part, got, total, per, sems):
    me = lax.axis_index(axis)

    def scatter():
        for d in range(1, n):
            k = (me + d) % n
            remote(part.at[pl.ds(k * per, per)], got.at[d - 1], sems.at[0], sems.at[1], {axis: k})

    def gather():
        drain(got, sems.at[1])
        mine = part[pl.ds(me * per, per)]
        for d in range(1, n):
            mine = mine + got[d - 1]
        own = total.at[pl.ds(me * per, per)]
        own[...] = mine
        for d in range(1, n):
            remote(own, own, sems.at[2], sems.at[3], {axis: (me + d) % n})

    def finish():
        drain(got, sems.at[0])
        drain(got, sems.at[2])
        drain(got, sems.at[3])

    return scatter, gather, finish


def power_kernel(
    sizes,
    momentum_ref,
    grad_ref,
    q_ref,
    power_ref,
    gram_ref,
    cross_ref,
    part,
    full,
    got_y,
    got_n,
    got_f,
    sum_y,
    sum_n,
    gram_part,
    gram_got,
    gram_total,
    cross_part,
    cross_got,
    cross_total,
    rs_send,
    rs_y,
    rs_n,
    rs_f,
    ag_send,
    ag_y,
    ag_n,
    ag_f,
    gram_sem,
    cross_sem,
):
    n_fsdp, n_f, n_n, n_y = sizes
    unit = TILES // (n_f * n_n * n_y)
    f_me, n_me, y_me = lax.axis_index("zf"), lax.axis_index("zn"), lax.axis_index("y")
    order = far_first(n_f)

    def chunk(f, y):
        return pl.ds((f * n_y + y) * (n_n * unit), n_n * unit)

    def tile(f, n, y):
        return pl.ds(((f * n_y + y) * n_n + n) * unit, unit)

    buffer = momentum_ref[...] + grad_ref[...].astype(jnp.float32)
    local = dot(buffer, q_ref[...], ((0,), (0,)))
    half = TILES // 2
    part[0:half] = local[:, 0:128].reshape(half, 8, 128)
    part[half:TILES] = local[:, 128:256].reshape(half, 8, 128)
    greet((("y", n_y), ("zn", n_n), ("zf", n_f), ("fsdp", n_fsdp)))

    for i, d in enumerate(order):
        f = (f_me + d) % n_f
        for e in range(1, n_y):
            y = (y_me + e) % n_y
            remote(part.at[chunk(f, y)], got_y.at[i, e - 1], rs_send.at[0], rs_y.at[i], {"y": y})

    def after_y(i):
        drain(got_y.at[i], rs_y.at[i])
        total = part[chunk((f_me + order[i]) % n_f, y_me)]
        for e in range(1, n_y):
            total = total + got_y[i, e - 1]
        sum_y[i] = total
        for e in range(1, n_n):
            n = (n_me + e) % n_n
            remote(
                sum_y.at[i, pl.ds(n * unit, unit)], got_n.at[i, e - 1], rs_send.at[1], rs_n.at[i], {"zn": n}
            )

    def after_n(i):
        drain(got_n.at[i], rs_n.at[i])
        total = sum_y[i, pl.ds(n_me * unit, unit)]
        for e in range(1, n_n):
            total = total + got_n[i, e - 1]
        sum_n[i] = total
        d = order[i]
        if d:
            remote(sum_n.at[i], got_f.at[d - 1], rs_send.at[2], rs_f, {"zf": (f_me + d) % n_f})

    lag = n_f // 2
    for i in range(n_f + lag):
        if i < n_f:
            after_y(i)
        if i >= lag:
            after_n(i - lag)
    drain(got_f, rs_f)
    total = sum_n[n_f - 1]
    for d in range(1, n_f):
        total = total + got_f[d - 1]

    own = full.at[tile(f_me, n_me, y_me)]
    own[...] = total
    for d in order[:-1]:
        remote(own, own, ag_send.at[0], ag_f.at[d], {"zf": (f_me + d) % n_f})

    def spread_n(d):
        f = (f_me - d + n_f) % n_f
        mine = full.at[tile(f, n_me, y_me)]
        if d:
            drain(mine, ag_f.at[d])
        for e in range(1, n_n):
            remote(mine, mine, ag_send.at[1], ag_n.at[d], {"zn": (n_me + e) % n_n})

    def spread_y(d):
        drain(full.at[0 : (n_n - 1) * unit], ag_n.at[d])
        mine = full.at[chunk((f_me - d + n_f) % n_f, y_me)]
        for e in range(1, n_y):
            remote(mine, mine, ag_send.at[2], ag_y, {"y": (y_me + e) % n_y})

    near = order[::-1]
    for i in range(n_f + 1):
        if i < n_f:
            spread_n(near[i])
        if i >= 1:
            spread_y(near[i - 1])
    drain(full.at[0 : TILES // n_y * (n_y - 1)], ag_y)

    left = full[0:half].reshape(half * 8, 128)
    right = full[half:TILES].reshape(half * 8, 128)
    whole = jnp.concatenate([left, right], axis=1)
    gram = dot(whole, whole, ((0,), (0,)))
    for i, (r, c) in enumerate(((0, 0), (0, 1), (1, 1))):
        block = gram[r * 128 : (r + 1) * 128, c * 128 : (c + 1) * 128]
        gram_part[i * 16 : (i + 1) * 16] = block.reshape(16, 8, 128)
    gram_scatter, gram_gather, gram_finish = sum_over(
        "fsdp", n_fsdp, gram_part, gram_got, gram_total, GRAM_TILES // n_fsdp, gram_sem
    )
    cross_scatter, cross_gather, cross_finish = sum_over(
        "fsdp", n_fsdp, cross_part, cross_got, cross_total, CROSS_TILES // n_fsdp, cross_sem
    )
    gram_scatter()
    cross = dot(buffer, whole, ((1,), (0,)))
    cross_part[0:14] = cross[:, 0:128].reshape(14, 8, 128)
    cross_part[14:28] = cross[:, 128:256].reshape(14, 8, 128)
    cross_part[28:32] = jnp.zeros((4, 8, 128), jnp.float32)
    cross_scatter()
    gram_gather()
    cross_gather()
    gram_finish()
    cross_finish()
    sent_y = TILES // n_y * (n_y - 1)
    drain(part.at[0:sent_y], rs_send.at[0])
    drain(got_n, rs_send.at[1])
    drain(got_f, rs_send.at[2])
    drain(got_f, ag_send.at[0])
    drain(got_n, ag_send.at[1])
    drain(part.at[0:sent_y], ag_send.at[2])
    power_ref[...] = full[...]
    gram_ref[...] = gram_total[...]
    cross_ref[...] = cross_total[...]


def eliminate(m):
    sub = lax.broadcasted_iota(jnp.int32, (8, 128), 0)
    lane = lax.broadcasted_iota(jnp.int32, (8, 128), 1)
    for p in range(16):
        lo, hi = 8 * p, 8 * p + 8
        rows = [m[lo:hi, 128 * c : 128 * (c + 1)] for c in range(3)]
        cols = [jnp.broadcast_to(rows[0][:, lo + j : lo + j + 1], (8, 128)) for j in range(8)]
        for j in range(8):
            scale = lax.rsqrt(cols[j][j : j + 1, :])
            factor = cols[j] * scale
            for k in range(j + 1, 8):
                cols[k] = cols[k] - factor * factor[k : k + 1, :]
            below = jnp.where(sub > j, factor, 0.0)
            for c in range(3):
                top = rows[c][j : j + 1, :] * scale
                rows[c] = jnp.where(sub == j, top, rows[c] - below * top)
        for c in range(3):
            m[lo:hi, 128 * c : 128 * (c + 1)] = rows[c]
        if p < 15:
            above = jnp.where(lane >= hi, rows[0], 0.0)
            change = dot(above, jnp.concatenate(rows, axis=1), ((0,), (0,)))
            m[hi:128, :] = m[hi:128, :] - change[hi:128, :]


def factor_kernel(
    power_ref, gram_ref, cross_ref, momentum_ref, grad_ref, right_ref, ortho_ref, square_ref, new_momentum_ref, m
):
    eye = (
        lax.broadcasted_iota(jnp.int32, (128, 128), 0) == lax.broadcasted_iota(jnp.int32, (128, 128), 1)
    ).astype(jnp.float32)
    m[:, 0:128] = gram_ref[0:16].reshape(128, 128)
    m[:, 128:256] = gram_ref[16:32].reshape(128, 128)
    m[:, 256:384] = eye
    eliminate(m)
    across, first = m[:, 128:256], m[:, 256:384]
    m[:, 0:128] = gram_ref[32:48].reshape(128, 128) - dot(across, across, ((0,), (0,)))
    m[:, 128:256] = -dot(across, first, ((0,), (0,)))
    m[:, 256:384] = eye
    eliminate(m)
    inverse = jnp.concatenate(
        [jnp.concatenate([first, jnp.zeros_like(first)], axis=1), m[:, 128:384]], axis=0
    )
    cross = jnp.concatenate([cross_ref[0:14].reshape(112, 128), cross_ref[14:28].reshape(112, 128)], axis=1)
    right = dot(cross, inverse, ((1,), (1,)))
    right_ref[...] = right
    square_ref[...] = jnp.sum(right * right, axis=0, keepdims=True)
    half = TILES // 2
    power = jnp.concatenate(
        [power_ref[0:half].reshape(half * 8, 128), power_ref[half:TILES].reshape(half * 8, 128)], axis=1
    )
    ortho = dot(power, inverse, ((1,), (1,)))
    ortho_ref[...] = ortho
    buffer = momentum_ref[...] + grad_ref[...].astype(jnp.float32)
    new_momentum_ref[...] = buffer - (1.0 - momentum_decay) * dot(right, ortho, ((1,), (1,)))


def norm_kernel(sizes, square_ref, out_ref, total, got_y, got_n, got_f, send, recv):
    axes = (("y", sizes[3]), ("zn", sizes[2]), ("zf", sizes[1]))
    greet(axes)
    value = square_ref[...]
    for i, ((axis, n), got) in enumerate(zip(axes, (got_y, got_n, got_f))):
        me = lax.axis_index(axis)
        total[i] = value
        for d in far_first(n)[:-1]:
            remote(total.at[i], got.at[d - 1], send.at[i], recv.at[i], {axis: (me + d) % n})
        drain(got, recv.at[i])
        for d in range(1, n):
            value = value + got[d - 1]
    for i, got in enumerate((got_y, got_n, got_f)):
        drain(got, send.at[i])
    out_ref[...] = value


def final_kernel(factor, weight_ref, right_ref, ortho_ref, square_ref, new_weight_ref, q_ref):
    q = right_ref[...] / (jnp.sqrt(square_ref[...]) + norm_eps)
    q_ref[...] = q
    update = dot(q, ortho_ref[...], ((1,), (1,)))
    new_weight_ref[...] = (weight_ref[...].astype(jnp.float32) - factor * update).astype(jnp.bfloat16)


def per_device(sizes, factor, weight, momentum, grad, q_prev):
    n_fsdp, n_f, n_n, n_y = sizes
    unit = TILES // (n_f * n_n * n_y)
    f32 = jnp.float32
    vmem = pl.BlockSpec(memory_space=pltpu.VMEM)

    def like(*shape):
        return jax.ShapeDtypeStruct(shape, f32)

    def tiles(*shape):
        return pltpu.VMEM((*shape, 8, 128), f32)

    dma = pltpu.SemaphoreType.DMA
    gram_per, cross_per = GRAM_TILES // n_fsdp, CROSS_TILES // n_fsdp
    power, gram, cross = pl.pallas_call(
        functools.partial(power_kernel, sizes),
        out_shape=(like(TILES, 8, 128), like(GRAM_TILES, 8, 128), like(CROSS_TILES, 8, 128)),
        in_specs=[vmem] * 3,
        out_specs=(vmem,) * 3,
        scratch_shapes=[
            tiles(TILES),
            tiles(TILES),
            tiles(n_f, n_y - 1, n_n * unit),
            tiles(n_f, n_n - 1, unit),
            tiles(n_f - 1, unit),
            tiles(n_f, n_n * unit),
            tiles(n_f, unit),
            tiles(GRAM_TILES),
            tiles(n_fsdp - 1, gram_per),
            tiles(GRAM_TILES),
            tiles(CROSS_TILES),
            tiles(n_fsdp - 1, cross_per),
            tiles(CROSS_TILES),
            dma((3,)),
            dma((n_f,)),
            dma((n_f,)),
            dma,
            dma((3,)),
            dma,
            dma((n_f,)),
            dma((n_f,)),
            dma((4,)),
            dma((4,)),
        ],
        compiler_params=pltpu.CompilerParams(collective_id=0, has_side_effects=True),
        name="power",
    )(momentum, grad, q_prev)
    rows, cols = momentum.shape
    right, ortho, square, new_momentum = pl.pallas_call(
        factor_kernel,
        out_shape=(like(rows, 256), like(cols, 256), like(1, 256), like(rows, cols)),
        in_specs=[vmem] * 5,
        out_specs=(vmem,) * 4,
        scratch_shapes=[pltpu.VMEM((128, 384), f32)],
        name="factor",
    )(power, gram, cross, momentum, grad)
    square = pl.pallas_call(
        functools.partial(norm_kernel, sizes),
        out_shape=like(1, 256),
        in_specs=[vmem],
        out_specs=vmem,
        scratch_shapes=[
            pltpu.VMEM((3, 1, 256), f32),
            pltpu.VMEM((n_y - 1, 1, 256), f32),
            pltpu.VMEM((n_n - 1, 1, 256), f32),
            pltpu.VMEM((n_f - 1, 1, 256), f32),
            dma((3,)),
            dma((3,)),
        ],
        compiler_params=pltpu.CompilerParams(collective_id=1, has_side_effects=True),
        name="norm",
    )(square)
    new_weight, q_new = pl.pallas_call(
        functools.partial(final_kernel, factor),
        out_shape=(jax.ShapeDtypeStruct((rows, cols), jnp.bfloat16), like(rows, 256)),
        in_specs=[vmem] * 4,
        out_specs=(vmem,) * 2,
        name="final",
    )(weight, right, ortho, square)
    return new_weight, new_momentum, q_new


def split_tensor(n):
    return (8, 4, 4) if n == 128 else (n // 4, 2, 2)


def solution(mesh):
    n_fsdp, n_tensor = mesh.shape["fsdp"], mesh.shape["tensor"]
    sizes = (n_fsdp, *split_tensor(n_tensor))
    torus = Mesh(mesh.devices.reshape(sizes), ("fsdp", *TENSOR))
    factor = step_rate * math.sqrt(14336 / 4096)
    return jax.shard_map(
        functools.partial(per_device, sizes, factor),
        mesh=torus,
        in_specs=(P(TENSOR, "fsdp"), P(TENSOR, "fsdp"), P(TENSOR, "fsdp"), P(TENSOR, None)),
        out_specs=(P(TENSOR, "fsdp"), P(TENSOR, "fsdp"), P(TENSOR, None)),
        check_vma=False,
    )
```

time: 422 us -> 137 us (0.32)
  the two profiles are of different devices: /device:TPU:4 before, /device:TPU:1 now
where the time goes in v1:
time: 137 us; the launch traced here: 136 us
  Pallas kernels  135 us (99%)
    pallas_call x1, Pallas kernels, per_device(): pl.pallas_call(functools.partial(power_kernel, sizes), out_shape=(like(TI...  84 us
    pallas_call x1, Pallas kernels, per_device(): pl.pallas_call(functools.partial(norm_kernel, sizes), out_shape=like(1, 2...  28.1 us
    pallas_call x1, Pallas kernels, per_device(): pl.pallas_call(factor_kernel, out_shape=(like(rows, 256), like(cols, 256)...  20.6 us

profile of v1, /device:TPU:1, one launch (start us, length us, event | category | flops | bytes accessed | tf_op | source)
XLA Modules:
  0.0 135.9 jit_solution(6771081702467322336)
XLA Ops:
  0.6 84.0 %power.1 = (f32[128,8,128]{2,1,0:T(8,128)}, f32[48,8,128]{2,1,0:T(8,128)}, f32[32,8,128]{2,1,0:T(8,128)}) custom-call(f32[112,512]{1,0:T(8,128)} %momentum_ref.3, bf16[112,512]{1,0:T(8,128)(2,1)} %grad_ref.3, f32[112,256]{1,0:T(8,128)} %q_ref.1), custom_call_target="tpu_custom_call" | custom-call | tf_op jit(solution)/shard_map/power/pallas_call | solution.py:337
  84.7 20.6 %factor.1 = (f32[112,256]{1,0:T(8,128)}, f32[512,256]{1,0:T(8,128)}, f32[1,256]{1,0:T(1,128)}, f32[112,512]{1,0:T(8,128)}) custom-call(f32[128,8,128]{2,1,0:T(8,128)} %get-tuple-element.12.power_ref, f32[48,8,128]{2,1,0:T(8,128)} %get-tuple-element.13.gram_ref, f32[32,8,128]{2,1,0:T(8,128)} %get-tuple-element.14.cross_ref, f32[112,512]{1,0:T(8,128)} %momentum_ref.3, ...), custom_call_target="tpu_custom_call" | custom-call | tf_op jit(solution)/shard_map/factor/pallas_call | solution.py:371
  105.3 28.1 %norm.1.square_ref = f32[1,256]{1,0:T(1,128)} custom-call(f32[1,256]{1,0:T(1,128)} %get-tuple-element.17.square_ref), custom_call_target="tpu_custom_call" | custom-call | tf_op jit(solution)/shard_map/norm/pallas_call | solution.py:379
  133.4 2.4 %final.1 = (bf16[112,512]{1,0:T(8,128)(2,1)}, f32[112,256]{1,0:T(8,128)}) custom-call(bf16[112,512]{1,0:T(8,128)(2,1)} %weight_ref.1, f32[112,256]{1,0:T(8,128)} %get-tuple-element.15.right_ref, f32[512,256]{1,0:T(8,128)} %get-tuple-element.16.ortho_ref, f32[1,256]{1,0:T(1,128)} %norm.1.square_ref), custom_call_target="tpu_custom_call" | custom-call | tf_op jit(solution)/shard_map/final/pallas_call | solution.py:395

commit v2 on v1

v2 whole, which is shorter than its diff:
```python
import functools
import math

import jax
import jax.numpy as jnp
from jax import lax
from jax.experimental import pallas as pl
from jax.experimental.pallas import tpu as pltpu
from jax.sharding import Mesh
from jax.sharding import PartitionSpec as P

TENSOR = ("zf", "zn", "y")
MESH_ID = pl.DeviceIdType.MESH
TILES = 128
GRAM_TILES = 48
CROSS_TILES = 32
PANEL = 32

momentum_decay = 0.95
step_rate = 0.02
norm_eps = 1e-06


def dot(left, right, dims):
    return lax.dot_general(
        left,
        right,
        (dims, ((), ())),
        precision=lax.Precision.HIGHEST,
        preferred_element_type=jnp.float32,
    )


def far_first(n):
    return sorted(range(1, n), key=lambda d: -min(d, n - d)) + [0]


def remote(src, dst, send, recv, device):
    copy = pltpu.make_async_remote_copy(
        src_ref=src,
        dst_ref=dst,
        send_sem=send,
        recv_sem=recv,
        device_id=device,
        device_id_type=MESH_ID,
    )
    copy.start()


def drain(ref, sem):
    pltpu.make_async_copy(ref, ref, sem).wait()


def greet(peers):
    barrier = pltpu.get_barrier_semaphore()
    for peer in peers:
        pl.semaphore_signal(barrier, inc=1, device_id=peer, device_id_type=MESH_ID)
    pl.semaphore_wait(barrier, len(peers))


def others(axis, n, steps=None):
    me = lax.axis_index(axis)
    return [{axis: (me + d) % n} for d in (range(1, n) if steps is None else steps)]


def sum_over(axis, n, part, got, total, per, sems):
    me = lax.axis_index(axis)

    def scatter():
        for d in range(1, n):
            k = (me + d) % n
            remote(part.at[pl.ds(k * per, per)], got.at[d - 1], sems.at[0], sems.at[1], {axis: k})

    def gather():
        drain(got, sems.at[1])
        mine = part[pl.ds(me * per, per)]
        for d in range(1, n):
            mine = mine + got[d - 1]
        own = total.at[pl.ds(me * per, per)]
        own[...] = mine
        for d in range(1, n):
            remote(own, own, sems.at[2], sems.at[3], {axis: (me + d) % n})

    def finish():
        drain(got, sems.at[0])
        drain(got, sems.at[2])
        drain(got, sems.at[3])

    return scatter, gather, finish


def eliminate(m):
    sub = lax.broadcasted_iota(jnp.int32, (8, 128), 0)
    lane = lax.broadcasted_iota(jnp.int32, (PANEL, 128), 1)
    groups = PANEL // 8

    def panel(p, carry):
        lo = pl.multiple_of(p * PANEL, PANEL)
        block = pltpu.roll(m[pl.ds(lo, PANEL), 0:128], (128 - lo) % 128, axis=1)
        rows = [
            [m[pl.ds(lo + 8 * v, 8), 128 * c : 128 * (c + 1)] for c in range(3)] for v in range(groups)
        ]
        cols = [
            {v: jnp.broadcast_to(block[8 * v : 8 * v + 8, j : j + 1], (8, 128)) for v in range(j // 8, groups)}
            for j in range(PANEL)
        ]
        for j in range(PANEL):
            top_group, s = j // 8, j % 8
            scale = lax.rsqrt(cols[j][top_group][s : s + 1, :])
            factor = {v: cols[j][v] * scale for v in range(top_group, groups)}
            for k in range(j + 1, PANEL):
                mult = factor[k // 8][k % 8 : k % 8 + 1, :]
                for v in range(k // 8, groups):
                    cols[k][v] = cols[k][v] - factor[v] * mult
            below = jnp.where(sub > s, factor[top_group], 0.0)
            for c in range(3):
                top = rows[top_group][c][s : s + 1, :] * scale
                rows[top_group][c] = jnp.where(sub == s, top, rows[top_group][c] - below * top)
                for v in range(top_group + 1, groups):
                    rows[v][c] = rows[v][c] - factor[v] * top
        done = jnp.concatenate([jnp.concatenate(row, axis=1) for row in rows], axis=0)
        m[pl.ds(lo, PANEL), :] = done
        above = jnp.where(lane >= lo + PANEL, done[:, 0:128], 0.0)
        m[...] = m[...] - dot(above, done, ((0,), (0,)))
        return carry

    lax.fori_loop(0, 128 // PANEL, panel, 0)


def step_kernel(
    sizes,
    factor,
    weight_ref,
    momentum_ref,
    grad_ref,
    q_ref,
    new_weight_ref,
    new_momentum_ref,
    new_q_ref,
    part,
    full,
    got_y,
    got_n,
    sum_y,
    sum_n,
    ring_left,
    ring_right,
    out_left,
    out_right,
    gram_part,
    gram_got,
    gram_total,
    cross_part,
    cross_got,
    cross_total,
    m,
    square,
    square_y,
    square_z,
    rs_send,
    rs_y,
    rs_n,
    rs_left,
    rs_right,
    ag_send,
    ag_y,
    ag_n,
    ag_f,
    gram_sem,
    cross_sem,
    square_sem,
):
    n_fsdp, n_f, n_n, n_y = sizes
    unit = TILES // (n_f * n_n * n_y)
    f_me, n_me, y_me = lax.axis_index("zf"), lax.axis_index("zn"), lax.axis_index("y")
    order = far_first(n_f)
    far = n_f // 2
    half = TILES // 2

    def chunk(f, y):
        return pl.ds((f * n_y + y) * (n_n * unit), n_n * unit)

    def tile(f, n, y):
        return pl.ds(((f * n_y + y) * n_n + n) * unit, unit)

    buffer = momentum_ref[...] + grad_ref[...].astype(jnp.float32)
    local = dot(buffer, q_ref[...], ((0,), (0,)))
    part[0:half] = local[:, 0:128].reshape(half, 8, 128)
    part[half:TILES] = local[:, 128:256].reshape(half, 8, 128)
    greet(
        others("y", n_y)
        + others("zn", n_n)
        + others("zf", n_f, sorted({1, n_f - 1}))
        + others("fsdp", n_fsdp)
    )

    for i, d in enumerate(order):
        f = (f_me + d) % n_f
        for e in range(1, n_y):
            y = (y_me + e) % n_y
            remote(part.at[chunk(f, y)], got_y.at[i, e - 1], rs_send.at[0], rs_y.at[i], {"y": y})

    def after_y(i):
        drain(got_y.at[i], rs_y.at[i])
        total = part[chunk((f_me + order[i]) % n_f, y_me)]
        for e in range(1, n_y):
            total = total + got_y[i, e - 1]
        sum_y[i] = total
        for e in range(1, n_n):
            n = (n_me + e) % n_n
            remote(
                sum_y.at[i, pl.ds(n * unit, unit)], got_n.at[i, e - 1], rs_send.at[1], rs_n.at[i], {"zn": n}
            )

    left = ((f_me + n_f - 1) % n_f, ring_left, out_left, rs_left, rs_send.at[2], far, lambda s: far + s)
    right = (
        (f_me + 1) % n_f,
        ring_right,
        out_right,
        rs_right,
        rs_send.at[3],
        n_f - 1 - far,
        lambda s: n_f - 1 - far - s,
    )

    def ring_step(way, s):
        peer, ring, out, recv, send, length, piece = way
        if s < length:
            value = sum_n[order.index(piece(s))]
            if s:
                drain(ring.at[s - 1], recv.at[s - 1])
                value = value + ring[s - 1]
            out[s] = value
            remote(out.at[s], ring.at[s], send, recv.at[s], {"zf": peer})

    def after_n(i):
        drain(got_n.at[i], rs_n.at[i])
        total = sum_y[i, pl.ds(n_me * unit, unit)]
        for e in range(1, n_n):
            total = total + got_n[i, e - 1]
        sum_n[i] = total
        for way in (left, right):
            if way[5] and order[i] == way[6](0):
                ring_step(way, 0)

    lag = n_f // 2
    for i in range(n_f + lag):
        if i < n_f:
            after_y(i)
        if i >= lag:
            after_n(i - lag)
    for s in range(1, far):
        ring_step(left, s)
        ring_step(right, s)
    total = sum_n[n_f - 1]
    for peer, ring, out, recv, send, length, piece in (left, right):
        if length:
            drain(ring.at[length - 1], recv.at[length - 1])
            total = total + ring[length - 1]

    own = full.at[tile(f_me, n_me, y_me)]
    own[...] = total
    for n in range(n_n):
        peer = {"zf": (f_me + far) % n_f, "zn": (n_me + n) % n_n}
        remote(own, own, ag_send.at[0], ag_f.at[far], peer)
    for d in order[1:-1]:
        remote(own, own, ag_send.at[0], ag_f.at[d], {"zf": (f_me + d) % n_f})

    def spread_n(d):
        mine = full.at[tile((f_me - d + n_f) % n_f, n_me, y_me)]
        if d:
            drain(mine, ag_f.at[d])
        for e in range(1, n_n):
            remote(mine, mine, ag_send.at[1], ag_n.at[d], {"zn": (n_me + e) % n_n})

    def spread_y(d):
        mine = full.at[chunk((f_me - d + n_f) % n_f, y_me)]
        if d == far:
            drain(mine, ag_f.at[d])
        else:
            drain(full.at[0 : (n_n - 1) * unit], ag_n.at[d])
        for e in range(1, n_y):
            remote(mine, mine, ag_send.at[2], ag_y, {"y": (y_me + e) % n_y})

    near = order[:0:-1]
    lag = min(3, n_f - 1)
    for i in range(n_f - 1 + lag):
        if i < n_f - 1:
            spread_n(near[i])
        if i == n_f:
            spread_y(far)
        if i >= lag:
            spread_y(near[i - lag])
    if n_f - 1 + lag <= n_f:
        spread_y(far)
    drain(full.at[0 : TILES // n_y * (n_y - 1)], ag_y)

    whole = jnp.concatenate(
        [full[0:half].reshape(half * 8, 128), full[half:TILES].reshape(half * 8, 128)], axis=1
    )
    gram = dot(whole, whole, ((0,), (0,)))
    for i, (r, c) in enumerate(((0, 0), (0, 1), (1, 1))):
        block = gram[r * 128 : (r + 1) * 128, c * 128 : (c + 1) * 128]
        gram_part[i * 16 : (i + 1) * 16] = block.reshape(16, 8, 128)
    gram_scatter, gram_gather, gram_finish = sum_over(
        "fsdp", n_fsdp, gram_part, gram_got, gram_total, GRAM_TILES // n_fsdp, gram_sem
    )
    cross_scatter, cross_gather, cross_finish = sum_over(
        "fsdp", n_fsdp, cross_part, cross_got, cross_total, CROSS_TILES // n_fsdp, cross_sem
    )
    gram_scatter()
    cross = dot(buffer, whole, ((1,), (0,)))
    cross_part[0:14] = cross[:, 0:128].reshape(14, 8, 128)
    cross_part[14:28] = cross[:, 128:256].reshape(14, 8, 128)
    cross_part[28:32] = jnp.zeros((4, 8, 128), jnp.float32)
    gram_gather()
    cross_scatter()
    gram_finish()

    eye = (
        lax.broadcasted_iota(jnp.int32, (128, 128), 0) == lax.broadcasted_iota(jnp.int32, (128, 128), 1)
    ).astype(jnp.float32)
    m[:, 0:128] = gram_total[0:16].reshape(128, 128)
    m[:, 128:256] = gram_total[16:32].reshape(128, 128)
    m[:, 256:384] = eye
    eliminate(m)
    cross_gather()
    across, first = m[:, 128:256], m[:, 256:384]
    m[:, 0:128] = gram_total[32:48].reshape(128, 128) - dot(across, across, ((0,), (0,)))
    m[:, 128:256] = -dot(across, first, ((0,), (0,)))
    m[:, 256:384] = eye
    eliminate(m)
    inverse = jnp.concatenate(
        [jnp.concatenate([first, jnp.zeros_like(first)], axis=1), m[:, 128:384]], axis=0
    )
    cross_finish()
    cross = jnp.concatenate(
        [cross_total[0:14].reshape(112, 128), cross_total[14:28].reshape(112, 128)], axis=1
    )
    right_factor = dot(cross, inverse, ((1,), (1,)))

    value = jnp.sum(right_factor * right_factor, axis=0, keepdims=True)
    square[0] = value
    for d in range(1, n_y):
        remote(square.at[0], square_y.at[d - 1], square_sem.at[0], square_sem.at[1], {"y": (y_me + d) % n_y})
    ortho = dot(whole, inverse, ((1,), (1,)))
    drain(square_y, square_sem.at[1])
    for d in range(1, n_y):
        value = value + square_y[d - 1]
    square[1] = value
    n_z = n_f * n_n
    z_me = f_me * n_n + n_me
    for d in far_first(n_z)[:-1]:
        z = (z_me + d) % n_z
        peer = {"zf": z // n_n, "zn": z % n_n}
        remote(square.at[1], square_z.at[d - 1], square_sem.at[2], square_sem.at[3], peer)
    new_momentum_ref[...] = buffer - (1.0 - momentum_decay) * dot(right_factor, ortho, ((1,), (1,)))

    drain(part.at[0 : TILES // n_y * (n_y - 1)], rs_send.at[0])
    drain(got_n, rs_send.at[1])
    for peer, ring, out, recv, send, length, piece in (left, right):
        if length:
            drain(out.at[0:length], send)
    drain(full.at[0 : (n_f - 2 + n_n) * unit], ag_send.at[0])
    drain(full.at[0 : (n_f - 1) * (n_n - 1) * unit], ag_send.at[1])
    drain(full.at[0 : TILES // n_y * (n_y - 1)], ag_send.at[2])
    drain(square_y, square_sem.at[0])
    drain(square_z, square_sem.at[3])
    drain(square_z, square_sem.at[2])
    for d in range(1, n_z):
        value = value + square_z[d - 1]
    q_new = right_factor / (jnp.sqrt(value) + norm_eps)
    new_q_ref[...] = q_new
    update = dot(q_new, ortho, ((1,), (1,)))
    new_weight_ref[...] = (weight_ref[...].astype(jnp.float32) - factor * update).astype(jnp.bfloat16)


def per_device(sizes, factor, weight, momentum, grad, q_prev):
    n_fsdp, n_f, n_n, n_y = sizes
    unit = TILES // (n_f * n_n * n_y)
    far = n_f // 2
    vmem = pl.BlockSpec(memory_space=pltpu.VMEM)
    dma = pltpu.SemaphoreType.DMA

    def tiles(*shape):
        return pltpu.VMEM((*shape, 8, 128), jnp.float32)

    def row(*shape):
        return pltpu.VMEM((*shape, 1, 256), jnp.float32)

    gram_per, cross_per = GRAM_TILES // n_fsdp, CROSS_TILES // n_fsdp
    return pl.pallas_call(
        functools.partial(step_kernel, sizes, factor),
        out_shape=(
            jax.ShapeDtypeStruct(weight.shape, jnp.bfloat16),
            jax.ShapeDtypeStruct(momentum.shape, jnp.float32),
            jax.ShapeDtypeStruct(q_prev.shape, jnp.float32),
        ),
        in_specs=[vmem] * 4,
        out_specs=(vmem,) * 3,
        scratch_shapes=[
            tiles(TILES),
            tiles(TILES),
            tiles(n_f, n_y - 1, n_n * unit),
            tiles(n_f, n_n - 1, unit),
            tiles(n_f, n_n * unit),
            tiles(n_f, unit),
            tiles(far, unit),
            tiles(far, unit),
            tiles(far, unit),
            tiles(far, unit),
            tiles(GRAM_TILES),
            tiles(n_fsdp - 1, gram_per),
            tiles(GRAM_TILES),
            tiles(CROSS_TILES),
            tiles(n_fsdp - 1, cross_per),
            tiles(CROSS_TILES),
            pltpu.VMEM((128, 384), jnp.float32),
            row(2),
            row(n_y - 1),
            row(n_f * n_n - 1),
            dma((4,)),
            dma((n_f,)),
            dma((n_f,)),
            dma((far,)),
            dma((far,)),
            dma((3,)),
            dma,
            dma((n_f,)),
            dma((n_f,)),
            dma((4,)),
            dma((4,)),
            dma((4,)),
        ],
        compiler_params=pltpu.CompilerParams(collective_id=0, has_side_effects=True),
        name="step",
    )(weight, momentum, grad, q_prev)


def split_tensor(n):
    return (8, 4, 4) if n == 128 else (n // 4, 2, 2)


def solution(mesh):
    n_fsdp, n_tensor = mesh.shape["fsdp"], mesh.shape["tensor"]
    sizes = (n_fsdp, *split_tensor(n_tensor))
    torus = Mesh(mesh.devices.reshape(sizes), ("fsdp", *TENSOR))
    factor = step_rate * math.sqrt(14336 / 4096)
    return jax.shard_map(
        functools.partial(per_device, sizes, factor),
        mesh=torus,
        in_specs=(P(TENSOR, "fsdp"), P(TENSOR, "fsdp"), P(TENSOR, "fsdp"), P(TENSOR, None)),
        out_specs=(P(TENSOR, "fsdp"), P(TENSOR, "fsdp"), P(TENSOR, None)),
        check_vma=False,
    )
```

time: 137 us -> 109 us (0.80)
  Pallas kernels: 135 us -> 105 us
  local copies, waits for them, and re-layouts: 0 us -> 3.22 us
    pallas_call x4 -> x1, Pallas kernels: 135 us -> 105 us  [per_device(): pl.pallas_call(functools.partial(step_kernel, sizes, factor), out_shape=(...]
    unnamed x0 -> x7, local copies, waits for them, and re-layouts: none -> 3.22 us
where the time goes in v2:
time: 109 us
  Pallas kernels  105 us (96%)
  local copies, waits for them, and re-layouts  3.22 us (3%)
    pallas_call x1, Pallas kernels, per_device(): pl.pallas_call(functools.partial(step_kernel, sizes, factor), out_shape=(...  105 us
    unnamed x7, local copies, waits for them, and re-layouts  3.22 us

profile of v2, /device:TPU:1, one launch (start us, length us, event | category | flops | bytes accessed | tf_op | source)
XLA Modules:
  0.0 108.9 jit_solution(16239781038401658076)
XLA Ops:
  0.6 105.1 %step.1 = (bf16[112,512]{1,0:T(8,128)(2,1)}, f32[112,512]{1,0:T(8,128)}, f32[112,256]{1,0:T(8,128)}) custom-call(bf16[112,512]{1,0:T(8,128)(2,1)} %weight_ref.1, f32[112,512]{1,0:T(8,128)} %momentum_ref.1, bf16[112,512]{1,0:T(8,128)(2,1)} %grad_ref.1, f32[112,256]{1,0:T(8,128)} %q_ref.1), custom_call_target="tpu_custom_call" | custom-call | tf_op jit(solution)/shard_map/step/pallas_call | solution.py:392
  105.7 0.0 copy-start
  105.7 1.6 %copy.10 = bf16[112,512]{1,0:T(8,128)(2,1)} copy(bf16[112,512]{1,0:T(8,128)(2,1)} %get-tuple-element.6) | data formatting | bytes 229376
  107.3 0.0 copy-done
  107.3 0.0 copy-start.1
  107.3 0.7 copy.11
  108.0 0.3 copy-done.1
  108.3 0.6 copy.12
Async XLA Ops:
  105.7 1.6 %copy-start = (f32[112,512]{1,0:T(8,128)S(1)}, f32[112,512]{1,0:T(8,128)}, u32[]{:S(2)}) copy-start(f32[112,512]{1,0:T(8,128)} %get-tuple-element.7) | copy-start | bytes 688132
  107.3 1.0 copy-start.1

commit v3 on v2

--- a/solution.py
+++ b/solution.py
@@ -55,7 +55,7 @@
     barrier = pltpu.get_barrier_semaphore()
     for peer in peers:
         pl.semaphore_signal(barrier, inc=1, device_id=peer, device_id_type=MESH_ID)
-    pl.semaphore_wait(barrier, len(peers))
+    return lambda: pl.semaphore_wait(barrier, len(peers))
 
 
 def others(axis, n, steps=None):
@@ -89,54 +89,57 @@
     return scatter, gather, finish
 
 
+def eliminate_panel(value, lo):
+    sub = lax.broadcasted_iota(jnp.int32, (8, 128), 0)
+    groups = PANEL // 8
+    rows = [[value[8 * v : 8 * v + 8, 128 * c : 128 * (c + 1)] for c in range(3)] for v in range(groups)]
+    cols = [
+        {v: jnp.broadcast_to(rows[v][0][:, lo + j : lo + j + 1], (8, 128)) for v in range(j // 8, groups)}
+        for j in range(PANEL)
+    ]
+    for j in range(PANEL):
+        top_group, s = j // 8, j % 8
+        scale = lax.rsqrt(cols[j][top_group][s : s + 1, :])
+        factor = {v: cols[j][v] * scale for v in range(top_group, groups)}
+        for k in range(j + 1, PANEL):
+            mult = factor[k // 8][k % 8 : k % 8 + 1, :]
+            for v in range(k // 8, groups):
+                cols[k][v] = cols[k][v] - factor[v] * mult
+        below = jnp.where(sub > s, factor[top_group], 0.0)
+        for c in range(3):
+            top = rows[top_group][c][s : s + 1, :] * scale
+            rows[top_group][c] = jnp.where(sub == s, top, rows[top_group][c] - below * top)
+            for v in range(top_group + 1, groups):
+                rows[v][c] = rows[v][c] - factor[v] * top
+    return jnp.concatenate([jnp.concatenate(row, axis=1) for row in rows], axis=0)
+
+
 def eliminate(m):
-    sub = lax.broadcasted_iota(jnp.int32, (8, 128), 0)
-    lane = lax.broadcasted_iota(jnp.int32, (PANEL, 128), 1)
-    groups = PANEL // 8
-
-    def panel(p, carry):
-        lo = pl.multiple_of(p * PANEL, PANEL)
-        block = pltpu.roll(m[pl.ds(lo, PANEL), 0:128], (128 - lo) % 128, axis=1)
-        rows = [
-            [m[pl.ds(lo + 8 * v, 8), 128 * c : 128 * (c + 1)] for c in range(3)] for v in range(groups)
-        ]
-        cols = [
-            {v: jnp.broadcast_to(block[8 * v : 8 * v + 8, j : j + 1], (8, 128)) for v in range(j // 8, groups)}
-            for j in range(PANEL)
-        ]
-        for j in range(PANEL):
-            top_group, s = j // 8, j % 8
-            scale = lax.rsqrt(cols[j][top_group][s : s + 1, :])
-            factor = {v: cols[j][v] * scale for v in range(top_group, groups)}
-            for k in range(j + 1, PANEL):
-                mult = factor[k // 8][k % 8 : k % 8 + 1, :]
-                for v in range(k // 8, groups):
-                    cols[k][v] = cols[k][v] - factor[v] * mult
-            below = jnp.where(sub > s, factor[top_group], 0.0)
-            for c in range(3):
-                top = rows[top_group][c][s : s + 1, :] * scale
-                rows[top_group][c] = jnp.where(sub == s, top, rows[top_group][c] - below * top)
-                for v in range(top_group + 1, groups):
-                    rows[v][c] = rows[v][c] - factor[v] * top
-        done = jnp.concatenate([jnp.concatenate(row, axis=1) for row in rows], axis=0)
-        m[pl.ds(lo, PANEL), :] = done
-        above = jnp.where(lane >= lo + PANEL, done[:, 0:128], 0.0)
-        m[...] = m[...] - dot(above, done, ((0,), (0,)))
-        return carry
-
-    lax.fori_loop(0, 128 // PANEL, panel, 0)
+    value = m[0:PANEL, :]
+    for lo in range(0, 128, PANEL):
+        hi, after = lo + PANEL, lo + 2 * PANEL
+        done = eliminate_panel(value, lo)
+        m[lo:hi, :] = done
+        if hi < 128:
+            value = m[hi:after, :] - dot(done[:, hi:after], done, ((0,), (0,)))
+        if after < 128:
+            m[after:128, :] = m[after:128, :] - dot(done[:, after:128], done, ((0,), (0,)))
 
 
 def step_kernel(
     sizes,
     factor,
+    weight_hbm,
+    momentum_hbm,
+    grad_hbm,
+    q_hbm,
+    new_weight_ref,
+    new_momentum_ref,
+    new_q_ref,
     weight_ref,
     momentum_ref,
     grad_ref,
     q_ref,
-    new_weight_ref,
-    new_momentum_ref,
-    new_q_ref,
     part,
     full,
     got_y,
@@ -169,6 +172,7 @@
     gram_sem,
     cross_sem,
     square_sem,
+    load_sem,
 ):
     n_fsdp, n_f, n_n, n_y = sizes
     unit = TILES // (n_f * n_n * n_y)
@@ -183,16 +187,27 @@
     def tile(f, n, y):
         return pl.ds(((f * n_y + y) * n_n + n) * unit, unit)
 
+    entered = greet(
+        others("y", n_y)
+        + others("zn", n_n)
+        + others("zf", n_f, sorted({1, n_f - 1}))
+        + others("fsdp", n_fsdp)
+    )
+    loads = [
+        pltpu.make_async_copy(src, dst, load_sem.at[i])
+        for i, (src, dst) in enumerate(
+            ((momentum_hbm, momentum_ref), (grad_hbm, grad_ref), (q_hbm, q_ref), (weight_hbm, weight_ref))
+        )
+    ]
+    for load in loads:
+        load.start()
+    for load in loads[:3]:
+        load.wait()
     buffer = momentum_ref[...] + grad_ref[...].astype(jnp.float32)
     local = dot(buffer, q_ref[...], ((0,), (0,)))
     part[0:half] = local[:, 0:128].reshape(half, 8, 128)
     part[half:TILES] = local[:, 128:256].reshape(half, 8, 128)
-    greet(
-        others("y", n_y)
-        + others("zn", n_n)
-        + others("zf", n_f, sorted({1, n_f - 1}))
-        + others("fsdp", n_fsdp)
-    )
+    entered()
 
     for i, d in enumerate(order):
         f = (f_me + d) % n_f
@@ -367,6 +382,7 @@
     drain(square_y, square_sem.at[0])
     drain(square_z, square_sem.at[3])
     drain(square_z, square_sem.at[2])
+    loads[3].wait()
     for d in range(1, n_z):
         value = value + square_z[d - 1]
     q_new = right_factor / (jnp.sqrt(value) + norm_eps)
@@ -375,11 +391,21 @@
     new_weight_ref[...] = (weight_ref[...].astype(jnp.float32) - factor * update).astype(jnp.bfloat16)
 
 
+def store_kernel(*refs):
+    values, outs, sem = refs[:3], refs[3:6], refs[6]
+    copies = [pltpu.make_async_copy(v, o, sem.at[i]) for i, (v, o) in enumerate(zip(values, outs))]
+    for copy in copies:
+        copy.start()
+    for copy in copies:
+        copy.wait()
+
+
 def per_device(sizes, factor, weight, momentum, grad, q_prev):
     n_fsdp, n_f, n_n, n_y = sizes
     unit = TILES // (n_f * n_n * n_y)
     far = n_f // 2
     vmem = pl.BlockSpec(memory_space=pltpu.VMEM)
+    hbm = pl.BlockSpec(memory_space=pltpu.HBM)
     dma = pltpu.SemaphoreType.DMA
 
     def tiles(*shape):
@@ -389,16 +415,21 @@
         return pltpu.VMEM((*shape, 1, 256), jnp.float32)
 
     gram_per, cross_per = GRAM_TILES // n_fsdp, CROSS_TILES // n_fsdp
-    return pl.pallas_call(
+    outs = (
+        jax.ShapeDtypeStruct(weight.shape, jnp.bfloat16),
+        jax.ShapeDtypeStruct(momentum.shape, jnp.float32),
+        jax.ShapeDtypeStruct(q_prev.shape, jnp.float32),
+    )
+    results = pl.pallas_call(
         functools.partial(step_kernel, sizes, factor),
-        out_shape=(
-            jax.ShapeDtypeStruct(weight.shape, jnp.bfloat16),
-            jax.ShapeDtypeStruct(momentum.shape, jnp.float32),
-            jax.ShapeDtypeStruct(q_prev.shape, jnp.float32),
-        ),
-        in_specs=[vmem] * 4,
+        out_shape=outs,
+        in_specs=[hbm] * 4,
         out_specs=(vmem,) * 3,
         scratch_shapes=[
+            pltpu.VMEM(weight.shape, weight.dtype),
+            pltpu.VMEM(momentum.shape, momentum.dtype),
+            pltpu.VMEM(grad.shape, grad.dtype),
+            pltpu.VMEM(q_prev.shape, q_prev.dtype),
             tiles(TILES),
             tiles(TILES),
             tiles(n_f, n_y - 1, n_n * unit),
@@ -431,10 +462,22 @@
             dma((4,)),
             dma((4,)),
             dma((4,)),
+            dma((4,)),
         ],
-        compiler_params=pltpu.CompilerParams(collective_id=0, has_side_effects=True),
+        compiler_params=pltpu.CompilerParams(
+            collective_id=0, has_side_effects=True, vmem_limit_bytes=24 << 20
+        ),
         name="step",
-    )(weight, momentum, grad, q_prev)
+    )(*(pltpu.with_memory_space_constraint(x, pltpu.HBM) for x in (weight, momentum, grad, q_prev)))
+    return pl.pallas_call(
+        store_kernel,
+        out_shape=outs,
+        in_specs=[vmem] * 3,
+        out_specs=(hbm,) * 3,
+        scratch_shapes=[dma((3,))],
+        compiler_params=pltpu.CompilerParams(vmem_limit_bytes=4 << 20),
+        name="store",
+    )(*results)
 
 
 def split_tensor(n):

time: 109 us -> 103 us (0.945)
  local copies, waits for them, and re-layouts: 3.22 us -> 0 us
  Pallas kernels: 105 us -> 102 us
    unnamed x7 -> x0, local copies, waits for them, and re-layouts: 3.22 us -> none
    pallas_call x1 -> x2, Pallas kernels: 105 us -> 102 us  [the longest x1 101 us: per_device(): pl.pallas_call(functools.partial(step_kernel, sizes, factor), out_shape=o...]
where the time goes in v3:
time: 103 us
  Pallas kernels  102 us (99%)
    pallas_call x1, Pallas kernels, per_device(): pl.pallas_call(functools.partial(step_kernel, sizes, factor), out_shape=o...  101 us

profile of v3, /device:TPU:1, one launch (start us, length us, event | category | flops | bytes accessed | tf_op | source)
XLA Modules:
  0.0 102.6 jit_solution(1002364013536097512)
XLA Ops:
  0.6 101.2 %step.1 = (bf16[112,512]{1,0:T(8,128)(2,1)S(1)}, f32[112,512]{1,0:T(8,128)S(1)}, f32[112,256]{1,0:T(8,128)S(1)}) custom-call(bf16[112,512]{1,0:T(8,128)(2,1)} %weight_hbm.1, f32[112,512]{1,0:T(8,128)} %momentum_hbm.1, bf16[112,512]{1,0:T(8,128)(2,1)} %grad_hbm.1, f32[112,256]{1,0:T(8,128)} %q_hbm.1), custom_call_target="tpu_custom_call" | custom-call | tf_op jit(solution)/shard_map/step/pallas_call | solution.py:423
  101.9 0.8 store.1

commit v4 on v3

--- a/solution.py
+++ b/solution.py
@@ -12,7 +12,8 @@
 TENSOR = ("zf", "zn", "y")
 MESH_ID = pl.DeviceIdType.MESH
 TILES = 128
-GRAM_TILES = 48
+FIRST_TILES = 32
+SECOND_TILES = 16
 CROSS_TILES = 32
 PANEL = 32
 
@@ -146,13 +147,13 @@
     got_n,
     sum_y,
     sum_n,
-    ring_left,
-    ring_right,
-    out_left,
-    out_right,
-    gram_part,
-    gram_got,
-    gram_total,
+    got_f,
+    first_part,
+    first_got,
+    first_total,
+    second_part,
+    second_got,
+    second_total,
     cross_part,
     cross_got,
     cross_total,
@@ -163,16 +164,17 @@
     rs_send,
     rs_y,
     rs_n,
-    rs_left,
-    rs_right,
+    rs_f,
     ag_send,
     ag_y,
     ag_n,
     ag_f,
-    gram_sem,
+    first_sem,
+    second_sem,
     cross_sem,
     square_sem,
     load_sem,
+    relay,
 ):
     n_fsdp, n_f, n_n, n_y = sizes
     unit = TILES // (n_f * n_n * n_y)
@@ -209,11 +211,26 @@
     part[half:TILES] = local[:, 128:256].reshape(half, 8, 128)
     entered()
 
+    def pass_on(k):
+        for peer in relayed[k]:
+            pl.semaphore_signal(relay.at[k], inc=1, device_id=peer, device_id_type=MESH_ID)
+
+    def passed_on(k):
+        pl.semaphore_wait(relay.at[k], len(relayed[k]))
+
+    steps = [1 << k for k in range(8) if 1 << k < far]
+    relayed = [others("zf", n_f, sorted({step, n_f - step})) for step in steps]
+    if steps:
+        pass_on(0)
+
     for i, d in enumerate(order):
         f = (f_me + d) % n_f
         for e in range(1, n_y):
             y = (y_me + e) % n_y
             remote(part.at[chunk(f, y)], got_y.at[i, e - 1], rs_send.at[0], rs_y.at[i], {"y": y})
+    for k in range(1, len(steps)):
+        passed_on(k - 1)
+        pass_on(k)
 
     def after_y(i):
         drain(got_y.at[i], rs_y.at[i])
@@ -223,30 +240,8 @@
         sum_y[i] = total
         for e in range(1, n_n):
             n = (n_me + e) % n_n
-            remote(
-                sum_y.at[i, pl.ds(n * unit, unit)], got_n.at[i, e - 1], rs_send.at[1], rs_n.at[i], {"zn": n}
-            )
-
-    left = ((f_me + n_f - 1) % n_f, ring_left, out_left, rs_left, rs_send.at[2], far, lambda s: far + s)
-    right = (
-        (f_me + 1) % n_f,
-        ring_right,
-        out_right,
-        rs_right,
-        rs_send.at[3],
-        n_f - 1 - far,
-        lambda s: n_f - 1 - far - s,
-    )
-
-    def ring_step(way, s):
-        peer, ring, out, recv, send, length, piece = way
-        if s < length:
-            value = sum_n[order.index(piece(s))]
-            if s:
-                drain(ring.at[s - 1], recv.at[s - 1])
-                value = value + ring[s - 1]
-            out[s] = value
-            remote(out.at[s], ring.at[s], send, recv.at[s], {"zf": peer})
+            share = sum_y.at[i, pl.ds(n * unit, unit)]
+            remote(share, got_n.at[i, e - 1], rs_send.at[1], rs_n.at[i], {"zn": n})
 
     def after_n(i):
         drain(got_n.at[i], rs_n.at[i])
@@ -254,24 +249,23 @@
         for e in range(1, n_n):
             total = total + got_n[i, e - 1]
         sum_n[i] = total
-        for way in (left, right):
-            if way[5] and order[i] == way[6](0):
-                ring_step(way, 0)
-
-    lag = n_f // 2
-    for i in range(n_f + lag):
-        if i < n_f:
-            after_y(i)
-        if i >= lag:
-            after_n(i - lag)
-    for s in range(1, far):
-        ring_step(left, s)
-        ring_step(right, s)
+        d = order[i]
+        if d:
+            remote(sum_n.at[i], got_f.at[i], rs_send.at[2], rs_f, {"zf": (f_me + d) % n_f})
+
+    waiting = list(range(n_f))
+    for i in range(min(n_f, 6)):
+        after_y(waiting.pop(0))
+    if steps:
+        passed_on(len(steps) - 1)
+    for i in range(n_f):
+        if i >= 3 and waiting:
+            after_y(waiting.pop(0))
+        after_n(i)
     total = sum_n[n_f - 1]
-    for peer, ring, out, recv, send, length, piece in (left, right):
-        if length:
-            drain(ring.at[length - 1], recv.at[length - 1])
-            total = total + ring[length - 1]
+    drain(got_f, rs_f)
+    for i in range(n_f - 1):
+        total = total + got_f[i]
 
     own = full.at[tile(f_me, n_me, y_me)]
     own[...] = total
@@ -314,34 +308,40 @@
         [full[0:half].reshape(half * 8, 128), full[half:TILES].reshape(half * 8, 128)], axis=1
     )
     gram = dot(whole, whole, ((0,), (0,)))
-    for i, (r, c) in enumerate(((0, 0), (0, 1), (1, 1))):
-        block = gram[r * 128 : (r + 1) * 128, c * 128 : (c + 1) * 128]
-        gram_part[i * 16 : (i + 1) * 16] = block.reshape(16, 8, 128)
-    gram_scatter, gram_gather, gram_finish = sum_over(
-        "fsdp", n_fsdp, gram_part, gram_got, gram_total, GRAM_TILES // n_fsdp, gram_sem
+    first_part[0:16] = gram[0:128, 0:128].reshape(16, 8, 128)
+    first_part[16:32] = gram[0:128, 128:256].reshape(16, 8, 128)
+    second_part[...] = gram[128:256, 128:256].reshape(16, 8, 128)
+    first_scatter, first_gather, first_finish = sum_over(
+        "fsdp", n_fsdp, first_part, first_got, first_total, FIRST_TILES // n_fsdp, first_sem
+    )
+    second_scatter, second_gather, second_finish = sum_over(
+        "fsdp", n_fsdp, second_part, second_got, second_total, SECOND_TILES // n_fsdp, second_sem
     )
     cross_scatter, cross_gather, cross_finish = sum_over(
         "fsdp", n_fsdp, cross_part, cross_got, cross_total, CROSS_TILES // n_fsdp, cross_sem
     )
-    gram_scatter()
+    first_scatter()
     cross = dot(buffer, whole, ((1,), (0,)))
     cross_part[0:14] = cross[:, 0:128].reshape(14, 8, 128)
     cross_part[14:28] = cross[:, 128:256].reshape(14, 8, 128)
     cross_part[28:32] = jnp.zeros((4, 8, 128), jnp.float32)
-    gram_gather()
+    first_gather()
+    second_scatter()
+    first_finish()
+    second_gather()
     cross_scatter()
-    gram_finish()
 
     eye = (
         lax.broadcasted_iota(jnp.int32, (128, 128), 0) == lax.broadcasted_iota(jnp.int32, (128, 128), 1)
     ).astype(jnp.float32)
-    m[:, 0:128] = gram_total[0:16].reshape(128, 128)
-    m[:, 128:256] = gram_total[16:32].reshape(128, 128)
+    m[:, 0:128] = first_total[0:16].reshape(128, 128)
+    m[:, 128:256] = first_total[16:32].reshape(128, 128)
     m[:, 256:384] = eye
     eliminate(m)
+    second_finish()
     cross_gather()
     across, first = m[:, 128:256], m[:, 256:384]
-    m[:, 0:128] = gram_total[32:48].reshape(128, 128) - dot(across, across, ((0,), (0,)))
+    m[:, 0:128] = second_total[...].reshape(128, 128) - dot(across, across, ((0,), (0,)))
     m[:, 128:256] = -dot(across, first, ((0,), (0,)))
     m[:, 256:384] = eye
     eliminate(m)
@@ -373,9 +373,7 @@
 
     drain(part.at[0 : TILES // n_y * (n_y - 1)], rs_send.at[0])
     drain(got_n, rs_send.at[1])
-    for peer, ring, out, recv, send, length, piece in (left, right):
-        if length:
-            drain(out.at[0:length], send)
+    drain(got_f, rs_send.at[2])
     drain(full.at[0 : (n_f - 2 + n_n) * unit], ag_send.at[0])
     drain(full.at[0 : (n_f - 1) * (n_n - 1) * unit], ag_send.at[1])
     drain(full.at[0 : TILES // n_y * (n_y - 1)], ag_send.at[2])
@@ -403,7 +401,6 @@
 def per_device(sizes, factor, weight, momentum, grad, q_prev):
     n_fsdp, n_f, n_n, n_y = sizes
     unit = TILES // (n_f * n_n * n_y)
-    far = n_f // 2
     vmem = pl.BlockSpec(memory_space=pltpu.VMEM)
     hbm = pl.BlockSpec(memory_space=pltpu.HBM)
     dma = pltpu.SemaphoreType.DMA
@@ -414,7 +411,6 @@
     def row(*shape):
         return pltpu.VMEM((*shape, 1, 256), jnp.float32)
 
-    gram_per, cross_per = GRAM_TILES // n_fsdp, CROSS_TILES // n_fsdp
     outs = (
         jax.ShapeDtypeStruct(weight.shape, jnp.bfloat16),
         jax.ShapeDtypeStruct(momentum.shape, jnp.float32),
@@ -436,25 +432,24 @@
             tiles(n_f, n_n - 1, unit),
             tiles(n_f, n_n * unit),
             tiles(n_f, unit),
-            tiles(far, unit),
-            tiles(far, unit),
-            tiles(far, unit),
-            tiles(far, unit),
-            tiles(GRAM_TILES),
-            tiles(n_fsdp - 1, gram_per),
-            tiles(GRAM_TILES),
+            tiles(n_f - 1, unit),
+            tiles(FIRST_TILES),
+            tiles(n_fsdp - 1, FIRST_TILES // n_fsdp),
+            tiles(FIRST_TILES),
+            tiles(SECOND_TILES),
+            tiles(n_fsdp - 1, SECOND_TILES // n_fsdp),
+            tiles(SECOND_TILES),
             tiles(CROSS_TILES),
-            tiles(n_fsdp - 1, cross_per),
+            tiles(n_fsdp - 1, CROSS_TILES // n_fsdp),
             tiles(CROSS_TILES),
             pltpu.VMEM((128, 384), jnp.float32),
             row(2),
             row(n_y - 1),
             row(n_f * n_n - 1),
-            dma((4,)),
+            dma((3,)),
             dma((n_f,)),
             dma((n_f,)),
-            dma((far,)),
-            dma((far,)),
+            dma,
             dma((3,)),
             dma,
             dma((n_f,)),
@@ -463,6 +458,8 @@
             dma((4,)),
             dma((4,)),
             dma((4,)),
+            dma((4,)),
+            pltpu.SemaphoreType.REGULAR((2,)),
         ],
         compiler_params=pltpu.CompilerParams(
             collective_id=0, has_side_effects=True, vmem_limit_bytes=24 << 20

time: 103 us -> 96.5 us (0.937)
  Pallas kernels: 102 us -> 95.7 us
    pallas_call x1, Pallas kernels: 101 us -> 94.9 us  [per_device(): pl.pallas_call(functools.partial(step_kernel, sizes, factor), out_shape=o...]
where the time goes in v4:
time: 96.5 us; the launch traced here: 96.3 us
  Pallas kernels  95.7 us (99%)
    pallas_call x1, Pallas kernels, per_device(): pl.pallas_call(functools.partial(step_kernel, sizes, factor), out_shape=o...  94.9 us

profile of v4, /device:TPU:1, one launch (start us, length us, event | category | flops | bytes accessed | tf_op | source)
XLA Modules:
  0.0 96.3 jit_solution(12919644090318223446)
XLA Ops:
  0.6 94.9 %step.1 = (bf16[112,512]{1,0:T(8,128)(2,1)S(1)}, f32[112,512]{1,0:T(8,128)S(1)}, f32[112,256]{1,0:T(8,128)S(1)}) custom-call(bf16[112,512]{1,0:T(8,128)(2,1)} %weight_hbm.1, f32[112,512]{1,0:T(8,128)} %momentum_hbm.1, bf16[112,512]{1,0:T(8,128)(2,1)} %grad_hbm.1, f32[112,256]{1,0:T(8,128)} %q_hbm.1), custom_call_target="tpu_custom_call" | custom-call | tf_op jit(solution)/shard_map/step/pallas_call | solution.py:419
  95.5 0.8 store.1

commit v5 on v4

--- a/solution.py
+++ b/solution.py
@@ -307,10 +307,9 @@
     whole = jnp.concatenate(
         [full[0:half].reshape(half * 8, 128), full[half:TILES].reshape(half * 8, 128)], axis=1
     )
-    gram = dot(whole, whole, ((0,), (0,)))
-    first_part[0:16] = gram[0:128, 0:128].reshape(16, 8, 128)
-    first_part[16:32] = gram[0:128, 128:256].reshape(16, 8, 128)
-    second_part[...] = gram[128:256, 128:256].reshape(16, 8, 128)
+    gram = dot(whole[:, 0:128], whole, ((0,), (0,)))
+    first_part[0:16] = gram[:, 0:128].reshape(16, 8, 128)
+    first_part[16:32] = gram[:, 128:256].reshape(16, 8, 128)
     first_scatter, first_gather, first_finish = sum_over(
         "fsdp", n_fsdp, first_part, first_got, first_total, FIRST_TILES // n_fsdp, first_sem
     )
@@ -321,6 +320,7 @@
         "fsdp", n_fsdp, cross_part, cross_got, cross_total, CROSS_TILES // n_fsdp, cross_sem
     )
     first_scatter()
+    second_part[...] = dot(whole[:, 128:256], whole[:, 128:256], ((0,), (0,))).reshape(16, 8, 128)
     cross = dot(buffer, whole, ((1,), (0,)))
     cross_part[0:14] = cross[:, 0:128].reshape(14, 8, 128)
     cross_part[14:28] = cross[:, 128:256].reshape(14, 8, 128)

time: 96.5 us -> 96.1 us (level)
  no operation moved by 1% of the time
where the time goes in v5:
time: 96.1 us; the launch traced here: 95.9 us
  Pallas kernels  95.3 us (99%)
    pallas_call x1, Pallas kernels, per_device(): pl.pallas_call(functools.partial(step_kernel, sizes, factor), out_shape=o...  94.5 us

profile of v5, /device:TPU:1, one launch (start us, length us, event | category | flops | bytes accessed | tf_op | source)
XLA Modules:
  0.0 95.9 jit_solution(12159595557666259663)
XLA Ops:
  0.6 94.5 %step.1 = (bf16[112,512]{1,0:T(8,128)(2,1)S(1)}, f32[112,512]{1,0:T(8,128)S(1)}, f32[112,256]{1,0:T(8,128)S(1)}) custom-call(bf16[112,512]{1,0:T(8,128)(2,1)} %weight_hbm.1, f32[112,512]{1,0:T(8,128)} %momentum_hbm.1, bf16[112,512]{1,0:T(8,128)(2,1)} %grad_hbm.1, f32[112,256]{1,0:T(8,128)} %q_hbm.1), custom_call_target="tpu_custom_call" | custom-call | tf_op jit(solution)/shard_map/step/pallas_call | solution.py:419
  95.2 0.8 store.1
